TPU v7x, 128 devices: a whole 4x4x4 slice. The times are simulated.
128 devices in a mesh: req: 16 (over z, y), mlp: 8 (over x, core).
Axes of the slice: x: 4, y: 4, z: 4, core: 2. Of those that a mesh axis runs over, the one named last changes fastest.
Arguments:
- hidden: bfloat16 [8192, 3584], P('req', 'mlp'), may hold values from -6 to 6
- query_heads: bfloat16 [8192, 3584], P('req', 'mlp'), may hold values from -4 to 4
- key_heads: bfloat16 [8192, 3584], P('req', 'mlp'), may hold values from -4 to 4
- value_heads: bfloat16 [8192, 3584], P('req', 'mlp'), may hold values from -6 to 6
- segment_ids: int32 [8192], P('req'), may hold values from 0 to 63, never falling along the last dimension, each value on 1 to 1024 neighbouring positions
- page_table: int32 [16, 32], P('req'), may hold values from 0 to 31, each once within a row
- mamba_conv_input: bfloat16 [8192, 7168], P('req', 'mlp'), may hold values from -6 to 6
- mamba_output_gate: bfloat16 [8192, 7168], P('req', 'mlp'), may hold values from -6 to 6
- state_input_projection: bfloat16 [8192, 128], P('req'), may hold values from -6 to 6
- state_output_projection: bfloat16 [8192, 128], P('req'), may hold values from -6 to 6
- discrete_step_size: float32 [8192, 112], P('req', 'mlp'), may hold values from 0.24 to 100, as said below
- head_decay_rate: float32 [112], P('mlp'), may hold values from 0.00024414062 to 0.05, as said below
- skip_gain: float32 [112], P('mlp'), may hold values from 0.5 to 2
- mamba_gated_norm_gain: float32 [7168], P('mlp'), may hold values from 0.1 to 1.9
- attn_proj: bfloat16 [3584, 3584], P('mlp'), may hold values from -0.09375 to 0.09375
- mamba_output_projection: bfloat16 [7168, 3584], P('mlp'), may hold values from -0.0625 to 0.0625
- mlp_norm_gain: float32 [3584], replicated, may hold values from 0.1 to 1.9
- gate_proj: bfloat16 [3584, 7168], P('req', 'mlp'), may hold values from -0.09375 to 0.09375
- up_proj: bfloat16 [3584, 7168], P('req', 'mlp'), may hold values from -0.09375 to 0.09375
- down_proj: bfloat16 [7168, 3584], P('mlp', 'req'), may hold values from -0.0625 to 0.0625
- next_norm_gain: float32 [3584], P('mlp'), may hold values from 0.1 to 1.9
Outputs:
- new_hidden: bfloat16 [8192, 3584], P('req', 'mlp')
- next_normed: bfloat16 [8192, 3584], P('req', 'mlp')
- kv_cache: bfloat16 [2, 16, 512, 3584], P(None, 'mlp', 'req')
Inputs may be any that keep to these rules, and one draw needn't show every extreme that they name: `segment_ids`: prompt ids never fall along the stream; a prompt has 1 to 1024 tokens and one has exactly 1024. `page_table`: each request group's row names every page of its pool once. `discrete_step_size`: Positive. `head_decay_rate`: Positive.
All inputs are finite; a program needn't handle non-finite values.
Results may differ from a plain program's by a relative error of at most 0.006.
Values may be sent and summed in bfloat16 or wider, within the bound.
No kernel may reach another device: no remote copies, remote signals or barrier semaphores. Data moves between devices by JAX's collectives and lax.ppermute only.
A program may use at most 128 MiB of HBM per device.

v0:
```python
import math
import jax
import jax.numpy as jnp
from jax import lax
from jax.sharding import PartitionSpec as P

HD = 224
MAMBA_HEAD_COUNT = 112
MAMBA_HEAD_SIZE = 64
STATE_SIZE = 64
STATE_GROUPS = 2
REACH = 2
PAGE = 16
EPSILON = 1e-05
exact_mode = lax.Precision.HIGHEST


def from_behind(value, axis, steps):
    count = lax.axis_size(axis)
    leading, last = (max(0, -steps), min(count, count - steps))
    return lax.ppermute(value, axis, [(source, source + steps) for source in range(leading, last)])


def entering(x, axis, combine, identity):
    devices, mine = (lax.axis_size(axis), lax.axis_index(axis))
    everything = jax.tree.map(lambda part: lax.all_gather(part, axis), x)
    start = jax.tree.map(
        lambda part, zero: jnp.broadcast_to(jnp.asarray(zero, part.dtype), part.shape), x, identity
    )

    def step(k, before):
        reached = k < mine
        new = combine(before, jax.tree.map(lambda part: part[k], everything))
        return jax.tree.map(lambda a, b: jnp.where(reached, a, b), new, before)

    return lax.fori_loop(0, devices, step, start)


def attend_rows(
    query_rows, segment_rows, pos_rows, all_keys, all_values, key_segs, key_pos, head_count
):
    row_total = query_rows.shape[0]
    key_total = all_keys.shape[0]
    query_split = query_rows.reshape(row_total, head_count, HD)
    key_split = all_keys.reshape(key_total, head_count, HD)
    value_split = all_values.reshape(key_total, head_count, HD)
    scores = jnp.einsum(
        "qhd,khd->hqk", query_split, key_split, preferred_element_type=jnp.float32
    ) * (1.0 / math.sqrt(HD))
    allowed = (segment_rows[:, None] == key_segs[None, :]) & (key_pos[None, :] <= pos_rows[:, None])
    scores = jnp.where(allowed[None, :, :], scores, -jnp.inf)
    top_score = jnp.max(scores, axis=2, keepdims=True)
    raised = jnp.exp(scores - top_score)
    weights = (raised / jnp.sum(raised, axis=2, keepdims=True)).astype(jnp.bfloat16)
    summed = jnp.einsum("hqk,khd->qhd", weights, value_split, preferred_element_type=jnp.float32)
    return summed.astype(jnp.bfloat16).reshape(row_total, head_count * HD)


def block_contributions(
    input_token_rows,
    input_proj_rows,
    output_proj_rows,
    step_size_rows,
    head_decay_rate,
    segment_rows,
    segment_prior_state,
    group_index,
    head_width,
):
    row_count = input_token_rows.shape[0]
    head_count = step_size_rows.shape[1]
    input_float = input_token_rows.astype(jnp.float32).reshape(row_count, head_count, head_width)
    b_float = input_proj_rows.astype(jnp.float32)
    c_float = output_proj_rows.astype(jnp.float32)
    running = jnp.cumsum(-step_size_rows * head_decay_rate[None, :], axis=0)
    positions = jnp.arange(row_count, dtype=jnp.int32)
    live = (segment_rows[:, None] == segment_rows[None, :]) & (
        positions[:, None] >= positions[None, :]
    )
    spread = running.T[:, :, None] - running.T[:, None, :]
    mixing = jnp.exp(jnp.where(live[None, :, :], spread, -1e30))
    inner = jnp.einsum("tgn,ugn->gtu", c_float, b_float, precision=exact_mode)
    driven = input_float * step_size_rows[:, :, None]
    local_output = jnp.einsum(
        "htu,uhp->thp", mixing * inner[group_index], driven, precision=exact_mode
    )
    b_per_head = b_float[:, group_index, :]
    output_proj_per_head = c_float[:, group_index, :]
    tail_rows = segment_rows == segment_rows[row_count - 1]
    tail_gain = jnp.where(
        tail_rows[:, None], jnp.exp(running[row_count - 1][None, :] - running), 0.0
    )
    state_local_part = jnp.einsum(
        "uh,uhp,uhn->hpn", tail_gain, driven, b_per_head, precision=exact_mode
    )
    decay_cumulative = jnp.where(
        segment_rows[row_count - 1] == segment_prior_state, jnp.exp(running[row_count - 1]), 0.0
    )
    entry_weighting = jnp.where(
        (segment_rows == segment_prior_state)[:, None], jnp.exp(running), 0.0
    )
    return (
        local_output,
        decay_cumulative,
        state_local_part,
        entry_weighting,
        input_float,
        output_proj_per_head,
    )


def finish(local_output, entry_weighting, input_float, output_proj_per_head, carry_in, skip_gain):
    carried = jnp.einsum("hpn,thn->thp", carry_in, output_proj_per_head, precision=exact_mode)
    result = (
        local_output
        + entry_weighting[:, :, None] * carried
        + skip_gain[None, :, None] * input_float
    )
    return result.reshape(result.shape[0], result.shape[1] * result.shape[2])


def merge_states(earlier, later):
    decay_early, state_early = earlier
    decay_late, state_late = later
    return (decay_early * decay_late, decay_late[:, None, None] * state_early + state_late)


def body(
    hidden,
    query_heads,
    key_heads,
    value_heads,
    segment_ids,
    page_table,
    mamba_conv_input,
    mamba_output_gate,
    state_input_projection,
    state_output_projection,
    discrete_step_size,
    head_decay_rate,
    skip_gain,
    mamba_gated_norm_gain,
    attn_proj,
    mamba_output_projection,
    mlp_norm_gain,
    gate_proj,
    up_proj,
    down_proj,
    next_norm_gain,
):
    row_count = query_heads.shape[0]
    head_count = query_heads.shape[1] // HD
    lane_count = hidden.shape[1]
    owner_index = lax.axis_index("req")
    column = lax.axis_index("mlp")
    first_row = owner_index * row_count
    lead_rows = REACH * row_count
    shifted_ids = segment_ids + 1
    key_parts = []
    value_parts = []
    segment_parts = []
    for distance in range(REACH, 0, -1):
        moved_ids = from_behind(shifted_ids, "req", distance)
        segment_parts.append(moved_ids - 1)
        moved_keys, moved_values = from_behind((key_heads, value_heads), "req", distance)
        key_parts.append(moved_keys)
        value_parts.append(moved_values)
    key_segs = jnp.concatenate(segment_parts + [segment_ids], axis=0)
    key_pos = first_row - lead_rows + jnp.arange(lead_rows + row_count, dtype=jnp.int32)
    segment_prior_state = segment_parts[-1][row_count - 1]
    all_keys = jnp.concatenate(key_parts + [key_heads], axis=0)
    all_values = jnp.concatenate(value_parts + [value_heads], axis=0)
    block_rows = min(row_count, 512)

    def one_block(block_index):
        first_local = block_index * block_rows
        pos_rows = first_row + first_local + jnp.arange(block_rows, dtype=jnp.int32)
        return attend_rows(
            query_heads, segment_ids, pos_rows, all_keys, all_values, key_segs, key_pos, head_count
        )

    attended = lax.map(one_block, jnp.arange(row_count // block_rows, dtype=jnp.int32)).reshape(
        row_count, head_count * HD
    )
    page_count = page_table.shape[1]
    key_pages = (
        key_heads.reshape(page_count, PAGE, head_count, HD)
        .transpose(2, 0, 1, 3)
        .reshape(head_count, page_count, PAGE * HD)
    )
    value_pages = (
        value_heads.reshape(page_count, PAGE, head_count, HD)
        .transpose(2, 0, 1, 3)
        .reshape(head_count, page_count, PAGE * HD)
    )
    stacked = jnp.stack([key_pages, value_pages])
    kv_cache = jnp.zeros_like(stacked).at[:, :, page_table[0]].set(stacked)
    mamba_heads = discrete_step_size.shape[1]
    group_values = MAMBA_HEAD_COUNT // STATE_GROUPS
    b_groups = state_input_projection.reshape(row_count, STATE_GROUPS, STATE_SIZE)
    c_groups = state_output_projection.reshape(row_count, STATE_GROUPS, STATE_SIZE)
    group_index = jnp.arange(mamba_heads, dtype=jnp.int32) % STATE_GROUPS
    (
        local_output,
        decay_cumulative,
        state_local_part,
        entry_weighting,
        input_float,
        output_proj_per_head,
    ) = block_contributions(
        mamba_conv_input,
        b_groups,
        c_groups,
        discrete_step_size,
        head_decay_rate,
        segment_ids,
        segment_prior_state,
        group_index,
        MAMBA_HEAD_SIZE,
    )
    unused_decay, carry_in = entering(
        (decay_cumulative, state_local_part),
        "req",
        merge_states,
        (jnp.ones_like(decay_cumulative), jnp.zeros_like(state_local_part)),
    )
    mamba_output = finish(
        local_output, entry_weighting, input_float, output_proj_per_head, carry_in, skip_gain
    )
    gated_output = mamba_output * jax.nn.silu(mamba_output_gate.astype(jnp.float32))
    grouped_values = gated_output.reshape(
        row_count, mamba_heads // STATE_GROUPS, STATE_GROUPS, MAMBA_HEAD_SIZE
    )
    group_squares = jnp.sum(grouped_values * grouped_values, axis=(1, 3))
    running_totals = lax.psum(group_squares, "mlp")
    inverse_group = lax.rsqrt(running_totals / (group_values * MAMBA_HEAD_SIZE) + EPSILON)
    mnormed = (
        (grouped_values * inverse_group[:, None, :, None]).reshape(
            row_count, mamba_heads * MAMBA_HEAD_SIZE
        )
        * mamba_gated_norm_gain[None, :]
    ).astype(jnp.bfloat16)
    projected = jnp.dot(attended, attn_proj, preferred_element_type=jnp.float32) + jnp.dot(
        mnormed, mamba_output_projection, preferred_element_type=jnp.float32
    )
    width_total = projected.shape[1]
    offset = column * lane_count
    own_part = lax.dynamic_slice_in_dim(projected, offset, lane_count, 1) + hidden.astype(
        jnp.float32
    )
    mixed_rows = lax.psum(lax.dynamic_update_slice_in_dim(projected, own_part, offset, 1), "mlp")
    mixed_share = lax.dynamic_slice_in_dim(mixed_rows, offset, lane_count, 1)
    inverse_root_mean = lax.rsqrt(jnp.mean(mixed_rows * mixed_rows, axis=1) + EPSILON)
    normed = (mixed_rows * inverse_root_mean[:, None] * mlp_norm_gain[None, :]).astype(jnp.bfloat16)
    gate_act = jnp.dot(
        normed,
        lax.all_gather(gate_proj, "req", axis=0, tiled=True),
        preferred_element_type=jnp.float32,
    )
    up_act = jnp.dot(
        normed,
        lax.all_gather(up_proj, "req", axis=0, tiled=True),
        preferred_element_type=jnp.float32,
    )
    latent_activation = (jax.nn.silu(gate_act) * up_act).astype(jnp.bfloat16)
    partial_value = jnp.dot(
        latent_activation,
        lax.all_gather(down_proj, "req", axis=1, tiled=True),
        preferred_element_type=jnp.float32,
    )
    mlp_share = lax.psum_scatter(partial_value, "mlp", scatter_dimension=1, tiled=True)
    new_hidden = (mixed_share + mlp_share).astype(jnp.bfloat16)
    widened = new_hidden.astype(jnp.float32)
    total_sq = lax.psum(jnp.sum(widened * widened, axis=1), "mlp")
    next_normed = (
        widened * lax.rsqrt(total_sq / width_total + EPSILON)[:, None] * next_norm_gain[None, :]
    ).astype(jnp.bfloat16)
    return (new_hidden, next_normed, kv_cache)


def solution(mesh):
    return jax.shard_map(
        body,
        mesh=mesh,
        in_specs=(
            P("req", "mlp"),
            P("req", "mlp"),
            P("req", "mlp"),
            P("req", "mlp"),
            P("req"),
            P("req", None),
            P("req", "mlp"),
            P("req", "mlp"),
            P("req", None),
            P("req", None),
            P("req", "mlp"),
            P("mlp"),
            P("mlp"),
            P("mlp"),
            P("mlp", None),
            P("mlp", None),
            P(),
            P("req", "mlp"),
            P("req", "mlp"),
            P("mlp", "req"),
            P("mlp"),
        ),
        out_specs=(P("req", "mlp"), P("req", "mlp"), P(None, "mlp", "req", None)),
        check_vma=False,
    )
```

profile of v0, /device:TPU:0, one launch (start us, length us, event | category | flops | bytes accessed | tf_op | source)
XLA Modules:
  0.0 616.1 jit_solution(2052999723825984348)
XLA Ops:
  8.7 3.6 collective-permute-start.3
  25.6 3.5 fusion.22
  29.2 5.4 collective-permute-start.2
  34.6 4.1 collective-permute-start.4
  38.7 4.3 collective-permute-start.5
  43.0 4.0 collective-permute-start
  47.0 3.6 collective-permute-start.1
  56.1 8.8 %gather_fusion = f32[14,512,512]{2,1,0:T(8,128)} fusion(f32[2,512,512]{2,1,0:T(8,128)} %fusion.59, s32[1024]{0:T(1024)} %copy-done.13), kind=kCustom, calls=%fused_computation | custom fusion | bytes 29360184 | tf_op jit(solution)/shard_map/gather | solution.py:85
  69.6 39.1 %all-gather.1 = f32[16,1,14]{2,1,0:T(1,128)S(1)} all-gather(f32[1,1,14]{2,1,0:T(1,128)S(1)} %bitcast.114), channel_id=1, replica_groups=mesh['req'=16,'mlp'=8] {'req'}, dimensions={0}, use_global_device_ids=true | all-gather | bytes 952 | tf_op jit(solution)/shard_map/all_gather | solution.py:26
  113.6 4.1 fusion.58
  117.7 6.2 %fusion.30 = bf16[2,224,512]{2,1,0:T(8,128)(2,1)} fusion(bf16[1536,2,224]{0,2,1:T(8,128)(2,1)} %bitcast.105, f32[2,512]{1,0:T(2,128)S(1)} %fusion.58, pred[512,1536]{0,1:T(8,128)(4,1)} %compare_and_fusion, bf16[1536,2,224]{0,2,1:T(8,128)(2,1)} %bitcast.104, bf16[512,2,224]{0,2,1:T(8,128)(2,1)} %bitcast.116), kind=kOutput, calls=%fused_computation.49 | convolution fusion | flops 1417382400 | bytes 4460544 | tf_op jit(solution)/shard_map/while/body/eval_jaxpr/hqk,khd->qhd/dot_general | solution.py:55
  123.9 43.8 %while.18 = (s32[]{:T(128)}, f32[14,64,64]{2,1,0:T(8,128)}, s32[]{:T(128)}, f32[16,14]{1,0:T(8,128)S(1)}, f32[16,14,64,64]{3,2,1,0:T(8,128)}, /*index=5*/s32[]{:T(128)}, s32[]{:T(128)}) while((s32[]{:T(128)}, f32[14,64,64]{2,1,0:T(8,128)}, s32[]{:T(128)}, f32[16,14]{1,0:T(8,128)S(1)}, f32[16,14,64,64]{3,2,1,0:T(8,128)}, ...), condition=%wide.region_5.6_spmd.clone, body=%wide.region_4.5_spmd.clone.sunk | while | flops 229380 | bytes 688401 | solution.py:36
  170.0 20.4 %fusion.21 = f32[512,14,64]{0,2,1:T(8,128)} fusion(f32[14,512,64]{1,2,0:T(8,128)S(1)} %fusion.37, f32[512,14,64]{0,2,1:T(8,128)S(1)} %bitcast.98, f32[14,512,512]{2,1,0:T(8,128)} %gather_fusion, f32[14,512]{1,0:T(8,128)S(1)} %bitcast.111, pred[512,512]{1,0:T(8,128)(4,1)S(1)} %copy-done.9, f32[14]{0:T(128)S(1)} %copy-done.18, f32[512,14]{0,1:T(8,128)S(1)} %copy-done.12, ...), kind=kOutput, calls=%fused_computation.38 | convolution fusion | flops 2831876096 | bytes 20533304 | tf_op jit(solution)/shard_map/htu,uhp->thp/dot_general | solution.py:84
  190.5 2.8 copy.80
  193.2 3.4 fusion.56
  196.7 2.8 copy.81
  201.1 12.4 %psum.21 = f32[512,2]{0,1:T(2,128)S(1)} all-reduce(f32[512,2]{0,1:T(2,128)S(1)} %reduce_sum.38), channel_id=1, replica_groups=mesh['req'=16,'mlp'=8] {'mlp'}, use_global_device_ids=true, to_apply=%region_7.8 | all-reduce | flops 1024 | bytes 8192 | tf_op jit(solution)/shard_map/psum | solution.py:235
  215.0 2.7 copy.82
  217.8 8.2 %fusion.35 = f32[512,3584]{1,0:T(8,128)S(1)} fusion(bf16[896,3584]{1,0:T(8,128)(2,1)} %param.38, f32[512,896]{1,0:T(8,128)} %copy.82, f32[896]{0:T(1024)S(1)} %copy-done.17, f32[512,896]{1,0:T(8,128)} %copy.80, bf16[512,896]{1,0:T(8,128)(2,1)} %param.30), kind=kOutput, calls=%fused_computation.57 | convolution fusion | flops 3292463104 | bytes 18353664 | tf_op jit(solution)/shard_map/dot_general | solution.py:243
  228.2 3.0 copy-done.2
  231.5 5.8 dynamic_update_slice.6
  239.3 88.7 %all-reduce.2.cloned.1.call-done = f32[512,3584]{1,0:T(8,128)} async-done(((f32[512,3584]{1,0:T(8,128)}), f32[512,3584]{1,0:T(8,128)}) %all-reduce.2.cloned.1.call-update) | async-done | bytes 7340048 | tf_op jit(solution)/shard_map/psum | solution.py:251
  328.1 3.6 multiply_reduce_fusion
  331.7 60.3 %all-gather.7.cloned.1.call-done = bf16[3584,896]{1,0:T(8,128)(2,1)} async-done(((bf16[224,896]{1,0:T(8,128)(2,1)}), bf16[3584,896]{1,0:T(8,128)(2,1)}) %all-gather.7.cloned.1.call-update) | async-done | bytes 6422544 | tf_op jit(solution)/shard_map/all_gather | solution.py:257
  392.0 8.4 %fusion.57 = f32[512,896]{1,0:T(8,128)S(1)} fusion(bf16[3584,896]{1,0:T(8,128)(2,1)} %all-gather.7.cloned.1.call-done, f32[512,3584]{1,0:T(8,128)} %all-reduce.2.cloned.1.call-done, f32[3584]{0:T(1024)S(1)} %copy-done.16, f32[512]{0:T(512)S(1)} %add_rsqrt_fusion.2), kind=kOutput, calls=%fused_computation.98 | convolution fusion | flops 3293839360 | bytes 15613952 | tf_op jit(solution)/shard_map/dot_general | solution.py:255
  400.5 55.1 %all-gather.11.cloned.1.call-done = bf16[896,3584]{0,1:T(8,128)(2,1)} async-done(((bf16[896,224]{0,1:T(8,128)(2,1)}), bf16[896,3584]{0,1:T(8,128)(2,1)}) %all-gather.11.cloned.1.call-update) | async-done | bytes 6422544 | tf_op jit(solution)/shard_map/all_gather | solution.py:268
  455.6 63.6 %all-gather.9.cloned.1.call-done = bf16[3584,896]{1,0:T(8,128)(2,1)} async-done(((bf16[224,896]{1,0:T(8,128)(2,1)}), bf16[3584,896]{1,0:T(8,128)(2,1)}) %all-gather.9.cloned.1.call-update) | async-done | bytes 6422544 | tf_op jit(solution)/shard_map/all_gather | solution.py:262
  519.2 17.7 %convolution_bitcast_fusion = f32[3584,512]{1,0:T(8,128)} fusion(bf16[896,3584]{0,1:T(8,128)(2,1)} %all-gather.11.cloned.1.call-done, f32[512,896]{1,0:T(8,128)S(1)} %fusion.57, bf16[3584,896]{1,0:T(8,128)(2,1)} %all-gather.9.cloned.1.call-done, f32[512,3584]{1,0:T(8,128)} %all-reduce.2.cloned.1.call-done, f32[3584]{0:T(1024)S(1)} %copy-done.16, ...), kind=kOutput, calls=%fused_computation.19 | convolution fusion | flops 6584926208 | bytes 29376512
  546.0 38.0 %reduce-scatter.4.cloned.1.call-done = f32[448,512]{1,0:T(8,128)} async-done(((f32[3584,512]{1,0:T(8,128)}), f32[448,512]{1,0:T(8,128)}) %reduce-scatter.4.cloned.1.call-update) | async-done | bytes 917520
  584.1 2.7 copy.96
  586.7 2.8 fusion.31
  589.6 13.2 %psum.23 = f32[512]{0:T(512)S(1)} all-reduce(f32[512]{0:T(512)S(1)} %get-tuple-element.167), channel_id=1, replica_groups=mesh['req'=16,'mlp'=8] {'mlp'}, use_global_device_ids=true, to_apply=%region_12.13 | all-reduce | flops 512 | bytes 4096 | tf_op jit(solution)/shard_map/psum | solution.py:274
  (151 shorter events, 86.1 us)
Async XLA Ops:
  7.2 218.8 %copy-start = (bf16[448,3584]{1,0:T(8,128)(2,1)S(1)}, bf16[448,3584]{1,0:T(8,128)(2,1)}, u32[]{:S(2)}) copy-start(bf16[448,3584]{1,0:T(8,128)(2,1)} %param.37) | copy-start | bytes 9633796
  7.2 116.7 %all-gather.13.cloned.1.call-start = ((), (), s32[]{:S(2)}) async-start(), calls=%async_computation.5 | async-start | bytes 7798784 | tf_op jit(solution)/shard_map/all_gather | solution.py:26
  8.7 12.3 %collective-permute-start.3 = (s32[512]{0:T(512)}, s32[512]{0:T(512)S(1)}, u32[]{:S(2)}, u32[]{:S(2)}) collective-permute-start(s32[512]{0:T(512)} %broadcast_add_fusion.3), channel_id=1, source_target_pairs={{0,8},{8,16},{16,24},{24,32},{32,40},{40,48},{48,56},{56,64},{64,7... | collective-permute-start | bytes 6152 | tf_op jit(solution)/shard_map/ppermute | solution.py:21
  14.5 6.4 %copy-start.13 = (s32[1024]{0:T(1024)}, s32[1024]{0:T(1024)S(1)}, u32[]{:S(2)}) copy-start(s32[1024]{0:T(1024)S(1)} %pad_clamp_fusion) | copy-start | bytes 12292
  19.4 3.4 copy-start.11
  19.4 6.2 copy-start.10
  29.1 298.9 %all-reduce.2.cloned.1.call-start = ((), (), s32[]{:S(2)}) async-start(), calls=%async_computation.1 | async-start | bytes 14680064 | tf_op jit(solution)/shard_map/psum | solution.py:251
  29.2 37.8 %collective-permute-start.2 = (s32[512]{0:T(512)}, s32[512]{0:T(512)}, u32[]{:S(2)}, u32[]{:S(2)}) collective-permute-start(s32[512]{0:T(512)} %broadcast_add_fusion.3), channel_id=1, source_target_pairs={{0,16},{8,24},{16,32},{24,40},{32,48},{40,56},{48,64},{56,72},{64,... | collective-permute-start | bytes 6152 | tf_op jit(solution)/shard_map/ppermute | solution.py:21
  34.6 74.2 %collective-permute-start.4 = (bf16[512,448]{0,1:T(8,128)(2,1)}, bf16[512,448]{0,1:T(8,128)(2,1)}, u32[]{:S(2)}, u32[]{:S(2)}) collective-permute-start(bf16[512,448]{0,1:T(8,128)(2,1)} %param.25), channel_id=1, source_target_pairs={{0,16},{8,24},{16,32},{24,40},{32,48},{40,56},{48,64},{56,72},{64,... | collective-permute-start | bytes 1376264 | tf_op jit(solution)/shard_map/ppermute | solution.py:21
  38.7 70.1 %collective-permute-start.5 = (bf16[512,448]{0,1:T(8,128)(2,1)}, bf16[512,448]{0,1:T(8,128)(2,1)}, u32[]{:S(2)}, u32[]{:S(2)}) collective-permute-start(bf16[512,448]{0,1:T(8,128)(2,1)} %param.25), channel_id=1, source_target_pairs={{0,8},{8,16},{16,24},{24,32},{32,40},{40,48},{48,56},{56,64},{64,7... | collective-permute-start | bytes 1376264 | tf_op jit(solution)/shard_map/ppermute | solution.py:21
  43.0 68.3 %collective-permute-start = (bf16[512,448]{0,1:T(8,128)(2,1)}, bf16[512,448]{0,1:T(8,128)(2,1)}, u32[]{:S(2)}, u32[]{:S(2)}) collective-permute-start(bf16[512,448]{0,1:T(8,128)(2,1)} %param.26), channel_id=1, source_target_pairs={{0,16},{8,24},{16,32},{24,40},{32,48},{40,56},{48,64},{56,72},{64,... | collective-permute-start | bytes 1376264 | tf_op jit(solution)/shard_map/ppermute | solution.py:21
  47.0 64.3 %collective-permute-start.1 = (bf16[512,448]{0,1:T(8,128)(2,1)}, bf16[512,448]{0,1:T(8,128)(2,1)}, u32[]{:S(2)}, u32[]{:S(2)}) collective-permute-start(bf16[512,448]{0,1:T(8,128)(2,1)} %param.26), channel_id=1, source_target_pairs={{0,8},{8,16},{16,24},{24,32},{32,40},{40,48},{48,56},{56,64},{64,7... | collective-permute-start | bytes 1376264 | tf_op jit(solution)/shard_map/ppermute | solution.py:21
  56.1 13.5 %copy-start.15 = (f32[14]{0:T(128)S(1)}, f32[14]{0:T(128)}, u32[]{:S(2)}) copy-start(f32[14]{0:T(128)} %get-tuple-element.156) | copy-start | bytes 172
  66.9 44.3 %copy-start.6 = (bf16[512,448]{0,1:T(8,128)(2,1)S(1)}, bf16[512,448]{0,1:T(8,128)(2,1)}, u32[]{:S(2)}) copy-start(bf16[512,448]{0,1:T(8,128)(2,1)} %param.26) | copy-start | bytes 1376260
  167.6 2.3 copy-start.3
  167.6 2.3 copy-start.9
  167.6 2.4 copy-start.12
  167.6 2.4 copy-start.18
  213.5 4.2 copy-start.17
  217.8 8.2 %copy-start.8 = (bf16[2,224,512]{2,1,0:T(8,128)(2,1)S(1)}, bf16[2,224,512]{2,1,0:T(8,128)(2,1)}, u32[]{:S(2)}) copy-start(bf16[2,224,512]{2,1,0:T(8,128)(2,1)} %fusion.30) | copy-start | bytes 1376260
  226.0 5.2 copy-start.4
  228.2 3.0 copy-start.2
  237.4 154.6 %all-gather.7.cloned.1.call-start = ((), (), s32[]{:S(2)}) async-start(), calls=%async_computation.2 | async-start | bytes 6823936 | tf_op jit(solution)/shard_map/all_gather | solution.py:257
  238.1 217.5 %all-gather.11.cloned.1.call-start = ((), (), s32[]{:S(2)}) async-start(), calls=%async_computation.4 | async-start | bytes 6823936 | tf_op jit(solution)/shard_map/all_gather | solution.py:268
  238.7 280.5 %all-gather.9.cloned.1.call-start = ((), (), s32[]{:S(2)}) async-start(), calls=%async_computation.3 | async-start | bytes 6823936 | tf_op jit(solution)/shard_map/all_gather | solution.py:262
  239.3 152.7 %copy-start.16 = (f32[3584]{0:T(1024)S(1)}, f32[3584]{0:T(1024)}, u32[]{:S(2)}) copy-start(f32[3584]{0:T(1024)} %param.39) | copy-start | bytes 43012
  239.3 344.8 %reduce-scatter.4.cloned.1.call-start = ((), (), s32[]{:S(2)}) async-start(), calls=%async_computation.6 | async-start | bytes 8257536
  536.9 1.0 copy-start.5
  536.9 1.2 copy-start.7
  540.0 2.0 copy-start.19
  584.1 20.8 %copy-start.14 = (f32[448]{0:T(512)S(1)}, f32[448]{0:T(512)}, u32[]{:S(2)}) copy-start(f32[448]{0:T(512)} %param.43) | copy-start | bytes 5380
  584.1 24.8 %copy-start.1 = (bf16[448,3584]{1,0:T(8,128)(2,1)S(1)}, bf16[448,3584]{1,0:T(8,128)(2,1)}, u32[]{:S(2)}) copy-start(bf16[448,3584]{1,0:T(8,128)(2,1)} %param.37) | copy-start | bytes 9633796
Sparse Core Ops, SparseCore 0:
  29.2 88.2 all-gather.12
  237.5 90.5 all-reduce.1
  330.2 61.7 all-gather.6
  394.0 61.5 all-gather.10
  457.6 61.5 all-gather.8
  537.1 46.9 reduce-scatter.3
where the time goes:
time: 626 us; the launch traced here: 616 us
  waiting for transfers between devices  308 us (49%)
  matrix products  75 us (12%)
  blocking collectives  64.8 us (10%)
  other arithmetic  61.3 us (10%)
  local copies, waits for them, and re-layouts  55 us (9%)
  starting transfers between devices  25.2 us (4%)
  between operations  16.2 us (3%)
  loops' own time  11.1 us (2%)
    psum x1, waiting for transfers between devices, body(): lax.psum(lax.dynamic_update_slice_in_dim(projected, own_part, offset, 1),...  88.7 us
    all_gather x1, waiting for transfers between devices, body(): lax.all_gather(up_proj, 'req', axis=0, tiled=True)  63.6 us
    all_gather x1, waiting for transfers between devices, body(): lax.all_gather(gate_proj, 'req', axis=0, tiled=True)  60.3 us
    all_gather x1, waiting for transfers between devices, body(): lax.all_gather(down_proj, 'req', axis=1, tiled=True)  55.1 us
    unnamed x7, waiting for transfers between devices  39.8 us
    all_gather x1, blocking collectives, entering(): everything = jax.tree.map(lambda part: lax.all_gather(part, axis), x)  39.1 us
    select_n x16, other arithmetic, step(): return jax.tree.map(lambda a, b: jnp.where(reached, a, b), new, before)  32.6 us
    ppermute x6, starting transfers between devices, from_behind(): lax.ppermute(value, axis, [(source, source + steps) for source in range(l...  25 us
  transfers between devices with their start and end apart: 12, of which 5 were waited for; matrix products, arithmetic and copies ran while one was open for 10% of the time, Pallas kernels for 0%

commit v1 on v0

--- a/solution.py
+++ b/solution.py
@@ -13,6 +13,11 @@
 PAGE = 16
 EPSILON = 1e-05
 exact_mode = lax.Precision.HIGHEST
+
+
+def exchange_gather(x, mesh_axis, d):
+    repeated = jnp.stack([x] * lax.axis_size(mesh_axis))
+    return jnp.concatenate(lax.all_to_all(repeated, mesh_axis, 0, 0), axis=d)
 
 
 def from_behind(value, axis, steps):
@@ -257,11 +262,7 @@
         lax.all_gather(gate_proj, "req", axis=0, tiled=True),
         preferred_element_type=jnp.float32,
     )
-    up_act = jnp.dot(
-        normed,
-        lax.all_gather(up_proj, "req", axis=0, tiled=True),
-        preferred_element_type=jnp.float32,
-    )
+    up_act = jnp.dot(normed, exchange_gather(up_proj, "req", 0), preferred_element_type=jnp.float32)
     latent_activation = (jax.nn.silu(gate_act) * up_act).astype(jnp.bfloat16)
     partial_value = jnp.dot(
         latent_activation,

time: 626 us -> 552 us (0.88)
  waiting for transfers between devices: 308 us -> 237 us
  loops' own time: 11.1 us -> 0.48 us
    all_gather x1 -> x0, waiting for transfers between devices: 63.6 us -> none  [body(): lax.all_gather(up_proj, 'req', axis=0, tiled=True)]
    another operation x1, loops' own time: 11.1 us -> 0.48 us  [entering(): return lax.fori_loop(0, devices, step, start)]
    psum x1, waiting for transfers between devices: 88.7 us -> 81.8 us  [body(): lax.psum(lax.dynamic_update_slice_in_dim(projected, own_part, offset, 1),...]
    unnamed x7 -> x6, waiting for transfers between devices: 39.8 us -> 39.3 us
    unnamed x51 -> x53, local copies, waits for them, and re-layouts: 16.2 us -> 16.2 us
  transfers between devices with their start and end apart: 12 -> 12, of which waited for: 5 -> 4; matrix products, arithmetic and copies ran while one was open for 10% -> 12% of each run, Pallas kernels for 0% -> 0%
where the time goes in v1:
time: 552 us; the launch traced here: 542 us
  waiting for transfers between devices  237 us (43%)
  matrix products  75 us (14%)
  blocking collectives  64.8 us (12%)
  other arithmetic  61.3 us (11%)
  local copies, waits for them, and re-layouts  58.2 us (11%)
  starting transfers between devices  29.9 us (5%)
  between operations  15.7 us (3%)
    psum x1, waiting for transfers between devices, body(): lax.psum(lax.dynamic_update_slice_in_dim(projected, own_part, offset, 1),...  81.8 us
    all_gather x1, waiting for transfers between devices, body(): lax.all_gather(gate_proj, 'req', axis=0, tiled=True)  60.6 us
    all_gather x1, waiting for transfers between devices, body(): lax.all_gather(down_proj, 'req', axis=1, tiled=True)  55.1 us
    unnamed x6, waiting for transfers between devices  39.3 us
    all_gather x1, blocking collectives, entering(): everything = jax.tree.map(lambda part: lax.all_gather(part, axis), x)  39.1 us
    select_n x16, other arithmetic, step(): return jax.tree.map(lambda a, b: jnp.where(reached, a, b), new, before)  32.6 us
    ppermute x6, starting transfers between devices, from_behind(): lax.ppermute(value, axis, [(source, source + steps) for source in range(l...  25 us
    dot_general x1, matrix products, block_contributions(): jnp.einsum('htu,uhp->thp', mixing * inner[group_index], driven, precision...  20.4 us
  transfers between devices with their start and end apart: 12, of which 4 were waited for; matrix products, arithmetic and copies ran while one was open for 12% of the time, Pallas kernels for 0%

profile of v1, /device:TPU:0, one launch (start us, length us, event | category | flops | bytes accessed | tf_op | source)
XLA Modules:
  0.0 542.2 jit_solution(3436221262910892269)
XLA Ops:
  8.7 3.6 collective-permute-start.3
  25.6 3.5 fusion.22
  29.2 5.4 collective-permute-start.2
  34.6 4.1 collective-permute-start.4
  38.7 4.3 collective-permute-start.5
  43.0 4.0 collective-permute-start
  47.0 3.6 collective-permute-start.1
  56.1 8.8 %gather_fusion = f32[14,512,512]{2,1,0:T(8,128)} fusion(f32[2,512,512]{2,1,0:T(8,128)} %fusion.59, s32[1024]{0:T(1024)} %copy-done.14), kind=kCustom, calls=%fused_computation | custom fusion | bytes 29360184 | tf_op jit(solution)/shard_map/gather | solution.py:90
  69.6 39.1 %all-gather.1 = f32[16,1,14]{2,1,0:T(1,128)S(1)} all-gather(f32[1,1,14]{2,1,0:T(1,128)S(1)} %bitcast.115), channel_id=1, replica_groups=mesh['req'=16,'mlp'=8] {'req'}, dimensions={0}, use_global_device_ids=true | all-gather | bytes 952 | tf_op jit(solution)/shard_map/all_gather | solution.py:31
  113.6 4.1 fusion.58
  117.7 6.2 %fusion.30 = bf16[2,224,512]{2,1,0:T(8,128)(2,1)} fusion(bf16[1536,2,224]{0,2,1:T(8,128)(2,1)} %bitcast.106, f32[2,512]{1,0:T(2,128)S(1)} %fusion.58, pred[512,1536]{0,1:T(8,128)(4,1)} %compare_and_fusion, bf16[1536,2,224]{0,2,1:T(8,128)(2,1)} %bitcast.105, bf16[512,2,224]{0,2,1:T(8,128)(2,1)} %bitcast.117), kind=kOutput, calls=%fused_computation.49 | convolution fusion | flops 1417382400 | bytes 4460544 | tf_op jit(solution)/shard_map/while/body/eval_jaxpr/hqk,khd->qhd/dot_general | solution.py:60
  123.9 33.2 %while.18 = (s32[]{:T(128)}, f32[14,64,64]{2,1,0:T(8,128)}, s32[]{:T(128)}, f32[16,14]{1,0:T(8,128)S(1)}, f32[16,14,64,64]{3,2,1,0:T(8,128)}, /*index=5*/s32[]{:T(128)}, s32[]{:T(128)}) while((s32[]{:T(128)}, f32[14,64,64]{2,1,0:T(8,128)}, s32[]{:T(128)}, f32[16,14]{1,0:T(8,128)S(1)}, f32[16,14,64,64]{3,2,1,0:T(8,128)}, ...), condition=%wide.region_5.6_spmd.clone, body=%wide.region_4.5_spmd.clone.sunk | while | flops 229380 | bytes 688401 | solution.py:41
  159.4 20.4 %fusion.21 = f32[512,14,64]{0,2,1:T(8,128)} fusion(f32[14,512,64]{1,2,0:T(8,128)S(1)} %fusion.37, f32[512,14,64]{0,2,1:T(8,128)S(1)} %bitcast.99, f32[14,512,512]{2,1,0:T(8,128)} %gather_fusion, f32[14,512]{1,0:T(8,128)S(1)} %bitcast.112, pred[512,512]{1,0:T(8,128)(4,1)S(1)} %copy-done.10, f32[14]{0:T(128)S(1)} %copy-done.19, f32[512,14]{0,1:T(8,128)S(1)} %copy-done.13, ...), kind=kOutput, calls=%fused_computation.38 | convolution fusion | flops 2831876096 | bytes 20533304 | tf_op jit(solution)/shard_map/htu,uhp->thp/dot_general | solution.py:89
  179.9 2.8 copy.80
  182.6 3.4 fusion.56
  186.1 2.8 copy.81
  190.5 12.4 %psum.21 = f32[512,2]{0,1:T(2,128)S(1)} all-reduce(f32[512,2]{0,1:T(2,128)S(1)} %reduce_sum.38), channel_id=1, replica_groups=mesh['req'=16,'mlp'=8] {'mlp'}, use_global_device_ids=true, to_apply=%region_7.8 | all-reduce | flops 1024 | bytes 8192 | tf_op jit(solution)/shard_map/psum | solution.py:240
  204.4 2.9 copy.82
  207.3 8.2 %fusion.35 = f32[512,3584]{1,0:T(8,128)S(1)} fusion(bf16[896,3584]{1,0:T(8,128)(2,1)} %param.38, f32[512,896]{1,0:T(8,128)} %copy.82, f32[896]{0:T(1024)S(1)} %copy-done.18, f32[512,896]{1,0:T(8,128)} %copy.80, bf16[512,896]{1,0:T(8,128)(2,1)} %param.30), kind=kOutput, calls=%fused_computation.57 | convolution fusion | flops 3292463104 | bytes 18353664 | tf_op jit(solution)/shard_map/dot_general | solution.py:248
  217.8 3.0 copy-done.2
  221.1 5.8 %dynamic_update_slice.6 = f32[512,3584]{1,0:T(8,128)} dynamic-update-slice(f32[512,3584]{1,0:T(8,128)} %copy-done.2, f32[512,448]{1,0:T(8,128)S(1)} %convert_add_fusion, s32[]{:T(128)} %constant.100.clone.1, s32[]{:T(128)S(6)} %select_n.104) | dynamic-update-slice | bytes 1835012 | tf_op jit(solution)/shard_map/dynamic_update_slice | solution.py:256
  228.3 3.1 stack.4
  231.4 4.6 all-to-all-start
  236.1 81.8 %all-reduce.2.cloned.1.call-done = f32[512,3584]{1,0:T(8,128)} async-done(((f32[512,3584]{1,0:T(8,128)}), f32[512,3584]{1,0:T(8,128)}) %all-reduce.2.cloned.1.call-update) | async-done | bytes 7340048 | tf_op jit(solution)/shard_map/psum | solution.py:256
  317.9 3.6 multiply_reduce_fusion
  321.6 60.6 %all-gather.6.cloned.1.call-done = bf16[3584,896]{1,0:T(8,128)(2,1)} async-done(((bf16[224,896]{1,0:T(8,128)(2,1)}), bf16[3584,896]{1,0:T(8,128)(2,1)}) %all-gather.6.cloned.1.call-update) | async-done | bytes 6422544 | tf_op jit(solution)/shard_map/all_gather | solution.py:262
  382.2 8.5 %fusion.57 = f32[512,896]{1,0:T(8,128)S(1)} fusion(bf16[3584,896]{1,0:T(8,128)(2,1)} %all-gather.6.cloned.1.call-done, f32[512,3584]{1,0:T(8,128)} %all-reduce.2.cloned.1.call-done, f32[3584]{0:T(1024)S(1)} %copy-done.17, f32[512]{0:T(512)S(1)} %add_rsqrt_fusion.2), kind=kOutput, calls=%fused_computation.98 | convolution fusion | flops 3293839360 | bytes 15613952 | tf_op jit(solution)/shard_map/dot_general | solution.py:260
  390.6 55.1 %all-gather.8.cloned.1.call-done = bf16[896,3584]{0,1:T(8,128)(2,1)} async-done(((bf16[896,224]{0,1:T(8,128)(2,1)}), bf16[896,3584]{0,1:T(8,128)(2,1)}) %all-gather.8.cloned.1.call-update) | async-done | bytes 6422544 | tf_op jit(solution)/shard_map/all_gather | solution.py:269
  445.7 17.7 %convolution_bitcast_fusion = f32[3584,512]{1,0:T(8,128)} fusion(bf16[896,3584]{0,1:T(8,128)(2,1)} %all-gather.8.cloned.1.call-done, f32[512,896]{1,0:T(8,128)S(1)} %fusion.57, bf16[3584,896]{1,0:T(8,128)(2,1)} %bitcast.23, f32[512,3584]{1,0:T(8,128)} %all-reduce.2.cloned.1.call-done, f32[3584]{0:T(1024)S(1)} %copy-done.17, f32[512]{0:T(512)S(1)} %add_rsqrt_fusion.2), kind=kOutput, calls=%fused_computation.19 | convolution fusion | flops 6584926208 | bytes 29376512
  472.6 38.0 %reduce-scatter.4.cloned.1.call-done = f32[448,512]{1,0:T(8,128)} async-done(((f32[3584,512]{1,0:T(8,128)}), f32[448,512]{1,0:T(8,128)}) %reduce-scatter.4.cloned.1.call-update) | async-done | bytes 917520
  513.3 2.8 fusion.31
  516.1 13.2 %psum.23 = f32[512]{0:T(512)S(1)} all-reduce(f32[512]{0:T(512)S(1)} %get-tuple-element.167), channel_id=1, replica_groups=mesh['req'=16,'mlp'=8] {'mlp'}, use_global_device_ids=true, to_apply=%region_12.13 | all-reduce | flops 512 | bytes 4096 | tf_op jit(solution)/shard_map/psum | solution.py:275
  (153 shorter events, 88.2 us)
Async XLA Ops:
  7.2 208.4 %copy-start = (bf16[448,3584]{1,0:T(8,128)(2,1)S(1)}, bf16[448,3584]{1,0:T(8,128)(2,1)}, u32[]{:S(2)}) copy-start(bf16[448,3584]{1,0:T(8,128)(2,1)} %param.37) | copy-start | bytes 9633796
  7.2 116.7 %all-gather.10.cloned.1.call-start = ((), (), s32[]{:S(2)}) async-start(), calls=%async_computation.5 | async-start | bytes 7798784 | tf_op jit(solution)/shard_map/all_gather | solution.py:31
  8.7 12.3 %collective-permute-start.3 = (s32[512]{0:T(512)}, s32[512]{0:T(512)S(1)}, u32[]{:S(2)}, u32[]{:S(2)}) collective-permute-start(s32[512]{0:T(512)} %broadcast_add_fusion.3), channel_id=1, source_target_pairs={{0,8},{8,16},{16,24},{24,32},{32,40},{40,48},{48,56},{56,64},{64,7... | collective-permute-start | bytes 6152 | tf_op jit(solution)/shard_map/ppermute | solution.py:26
  14.5 6.4 %copy-start.14 = (s32[1024]{0:T(1024)}, s32[1024]{0:T(1024)S(1)}, u32[]{:S(2)}) copy-start(s32[1024]{0:T(1024)S(1)} %pad_clamp_fusion) | copy-start | bytes 12292
  19.4 3.4 copy-start.12
  19.4 6.2 %copy-start.11 = (f32[512,14]{0,1:T(8,128)S(1)}, f32[512,14]{0,1:T(8,128)}, u32[]{:S(2)}) copy-start(f32[512,14]{0,1:T(8,128)} %param.33) | copy-start | bytes 86020
  29.1 288.8 %all-reduce.2.cloned.1.call-start = ((), (), s32[]{:S(2)}) async-start(), calls=%async_computation.2 | async-start | bytes 14680064 | tf_op jit(solution)/shard_map/psum | solution.py:256
  29.2 37.8 %collective-permute-start.2 = (s32[512]{0:T(512)}, s32[512]{0:T(512)}, u32[]{:S(2)}, u32[]{:S(2)}) collective-permute-start(s32[512]{0:T(512)} %broadcast_add_fusion.3), channel_id=1, source_target_pairs={{0,16},{8,24},{16,32},{24,40},{32,48},{40,56},{48,64},{56,72},{64,... | collective-permute-start | bytes 6152 | tf_op jit(solution)/shard_map/ppermute | solution.py:26
  34.6 74.2 %collective-permute-start.4 = (bf16[512,448]{0,1:T(8,128)(2,1)}, bf16[512,448]{0,1:T(8,128)(2,1)}, u32[]{:S(2)}, u32[]{:S(2)}) collective-permute-start(bf16[512,448]{0,1:T(8,128)(2,1)} %param.25), channel_id=1, source_target_pairs={{0,16},{8,24},{16,32},{24,40},{32,48},{40,56},{48,64},{56,72},{64,... | collective-permute-start | bytes 1376264 | tf_op jit(solution)/shard_map/ppermute | solution.py:26
  38.7 70.1 %collective-permute-start.5 = (bf16[512,448]{0,1:T(8,128)(2,1)}, bf16[512,448]{0,1:T(8,128)(2,1)}, u32[]{:S(2)}, u32[]{:S(2)}) collective-permute-start(bf16[512,448]{0,1:T(8,128)(2,1)} %param.25), channel_id=1, source_target_pairs={{0,8},{8,16},{16,24},{24,32},{32,40},{40,48},{48,56},{56,64},{64,7... | collective-permute-start | bytes 1376264 | tf_op jit(solution)/shard_map/ppermute | solution.py:26
  43.0 68.3 %collective-permute-start = (bf16[512,448]{0,1:T(8,128)(2,1)}, bf16[512,448]{0,1:T(8,128)(2,1)}, u32[]{:S(2)}, u32[]{:S(2)}) collective-permute-start(bf16[512,448]{0,1:T(8,128)(2,1)} %param.26), channel_id=1, source_target_pairs={{0,16},{8,24},{16,32},{24,40},{32,48},{40,56},{48,64},{56,72},{64,... | collective-permute-start | bytes 1376264 | tf_op jit(solution)/shard_map/ppermute | solution.py:26
  47.0 64.3 %collective-permute-start.1 = (bf16[512,448]{0,1:T(8,128)(2,1)}, bf16[512,448]{0,1:T(8,128)(2,1)}, u32[]{:S(2)}, u32[]{:S(2)}) collective-permute-start(bf16[512,448]{0,1:T(8,128)(2,1)} %param.26), channel_id=1, source_target_pairs={{0,8},{8,16},{16,24},{24,32},{32,40},{40,48},{48,56},{56,64},{64,7... | collective-permute-start | bytes 1376264 | tf_op jit(solution)/shard_map/ppermute | solution.py:26
  56.1 13.5 %copy-start.16 = (f32[14]{0:T(128)S(1)}, f32[14]{0:T(128)}, u32[]{:S(2)}) copy-start(f32[14]{0:T(128)} %get-tuple-element.156) | copy-start | bytes 172
  66.9 44.3 %copy-start.6 = (bf16[512,448]{0,1:T(8,128)(2,1)S(1)}, bf16[512,448]{0,1:T(8,128)(2,1)}, u32[]{:S(2)}) copy-start(bf16[512,448]{0,1:T(8,128)(2,1)} %param.26) | copy-start | bytes 1376260
  157.1 2.3 copy-start.3
  157.1 2.3 copy-start.10
  157.1 2.4 copy-start.13
  157.1 2.4 copy-start.19
  203.0 4.4 copy-start.18
  207.3 8.2 %copy-start.8 = (bf16[2,224,512]{2,1,0:T(8,128)(2,1)S(1)}, bf16[2,224,512]{2,1,0:T(8,128)(2,1)}, u32[]{:S(2)}) copy-start(bf16[2,224,512]{2,1,0:T(8,128)(2,1)} %fusion.30) | copy-start | bytes 1376260
  215.5 5.2 copy-start.4
  217.8 3.0 copy-start.2
  226.9 1.3 copy-start.9
  227.0 155.2 %all-gather.6.cloned.1.call-start = ((), (), s32[]{:S(2)}) async-start(), calls=%async_computation.3 | async-start | bytes 6823936 | tf_op jit(solution)/shard_map/all_gather | solution.py:262
  227.7 218.0 %all-gather.8.cloned.1.call-start = ((), (), s32[]{:S(2)}) async-start(), calls=%async_computation.4 | async-start | bytes 6823936 | tf_op jit(solution)/shard_map/all_gather | solution.py:269
  231.4 159.3 %all-to-all-start = ((bf16[16,224,896]{2,1,0:T(8,128)(2,1)}), bf16[16,224,896]{2,1,0:T(8,128)(2,1)}, u32[]{:S(2)}, u32[]{:S(2)}) async-start(bf16[16,224,896]{2,1,0:T(8,128)(2,1)} %stack.4), calls=%async_computation | async-start | bytes 12845056 | tf_op jit(solution)/shard_map/all_to_all | solution.py:20
  236.0 146.1 %copy-start.17 = (f32[3584]{0:T(1024)S(1)}, f32[3584]{0:T(1024)}, u32[]{:S(2)}) copy-start(f32[3584]{0:T(1024)} %param.39) | copy-start | bytes 43012
  236.1 274.6 %reduce-scatter.4.cloned.1.call-start = ((), (), s32[]{:S(2)}) async-start(), calls=%async_computation.6 | async-start | bytes 8257536
  463.5 1.2 copy-start.7
  466.5 2.0 copy-start.20
  510.6 20.8 %copy-start.15 = (f32[448]{0:T(512)S(1)}, f32[448]{0:T(512)}, u32[]{:S(2)}) copy-start(f32[448]{0:T(512)} %param.43) | copy-start | bytes 5380
  510.6 24.8 %copy-start.1 = (bf16[448,3584]{1,0:T(8,128)(2,1)S(1)}, bf16[448,3584]{1,0:T(8,128)(2,1)}, u32[]{:S(2)}) copy-start(bf16[448,3584]{1,0:T(8,128)(2,1)} %param.37) | copy-start | bytes 9633796
  (1 other events, 1.0 us)
Sparse Core Ops, SparseCore 0:
  29.2 88.2 all-gather.9
  227.1 90.7 all-reduce.1
  320.1 62.0 all-gather.5
  384.1 61.5 all-gather.7
  463.6 46.9 reduce-scatter.3
